TPU v7x, 32 devices: a whole 2x2x4 slice. The times are simulated.
32 devices in a mesh: cfg: 2 (over y), tm: 4 (over z), space: 2 (over x), spin: 2 (over core).
Axes of the slice: x: 2, y: 2, z: 4, core: 2. Of those that a mesh axis runs over, the one named last changes fastest.
Arguments:
- eigenvectors: bfloat16 [8, 2, 3, 16, 2, 2, 128], P(('cfg', 'tm'), None, None, 'space'), parts along dimension 0, may hold values from -6 to 6
- gauge_links: bfloat16 [8, 3, 2, 3, 3, 16, 4], P(('cfg', 'tm'), None, None, None, None, 'space'), parts along dimension 0, may hold values from -2.4375 to 2.4375
- perambulators: bfloat16 [8, 512, 1024], P(('cfg', 'tm'), ('space', 'spin')), parts along dimension 0, may hold values from -0.1875 to 0.1875
- source_times: int32 [16], replicated, may hold values from 0 to 3
- insert_offsets: int32 [4], replicated, may hold values from 0 to 2
- derivative_dirs: int32 [3], replicated, may hold values from 0 to 2, each once
Outputs:
- elementals: float32 [8, 128, 3, 2, 128], P(('cfg', 'tm'), 'space', None, None, 'spin'), parts along dimension 0
- chain_products: bfloat16 [8, 512, 1024], P(('cfg', 'tm'), ('space', 'spin')), parts along dimension 0
- correlator: float32 [32, 2], P('cfg'), parts along dimension 0
There are 2 independent parts, one for each index of `cfg`. A program takes and returns all parts, laid end to end along the dimension named above; an argument that names none is the same for every part. Nothing has to cross between parts.
Inputs may be any that keep to these rules, and one draw needn't show every extreme that they name: `derivative_dirs`: each of 0, 1, 2 appears once.
All inputs are finite; a program needn't handle non-finite values.
Results may differ from a plain program's by a relative error of at most 0.012.
Values may be sent and summed in bfloat16 or wider, within the bound.
A program may use at most 64 MiB of HBM per device.

v0:
```python
import math

import jax
import jax.numpy as jnp
import numpy as np
from jax import lax
from jax.sharding import PartitionSpec as P


def shifted(block, axis, distance):
    devices = range(lax.axis_size(axis))
    route = [((i - distance) % len(devices), i) for i in devices]
    return lax.ppermute(block, axis, route)


def gamma_tables():
    sigma_real = np.zeros((3, 2, 2), np.float32)
    sigma_imag = np.zeros((3, 2, 2), np.float32)
    sigma_real[0] = [[0.0, 1.0], [1.0, 0.0]]
    sigma_imag[1] = [[0.0, -1.0], [1.0, 0.0]]
    sigma_real[2] = [[1.0, 0.0], [0.0, -1.0]]
    gamma_real = np.zeros((3, 4, 4), np.float32)
    gamma_imag = np.zeros((3, 4, 4), np.float32)
    gamma_real[:, 0:2, 2:4] = sigma_imag
    gamma_imag[:, 0:2, 2:4] = -sigma_real
    gamma_real[:, 2:4, 0:2] = -sigma_imag
    gamma_imag[:, 2:4, 0:2] = sigma_real
    return (gamma_real, gamma_imag)


def color_product(matrix, vectors):
    return jnp.sum(matrix[:, :, :, :, :, None] * vectors[None], axis=1)


def times_links(link_field, vectors):
    real_part = color_product(link_field[0], vectors[0]) - color_product(link_field[1], vectors[1])
    imag_part = color_product(link_field[0], vectors[1]) + color_product(link_field[1], vectors[0])
    return jnp.stack([real_part, imag_part])


def times_adjoint(link_field, vectors):
    swapped = jnp.swapaxes(link_field, 1, 2)
    real_part = color_product(swapped[0], vectors[0]) + color_product(swapped[1], vectors[1])
    imag_part = color_product(swapped[0], vectors[1]) - color_product(swapped[1], vectors[0])
    return jnp.stack([real_part, imag_part])


def block_matrix(real_part, imag_part):
    upper_half = jnp.concatenate([real_part, imag_part], axis=1)
    lower_half = jnp.concatenate([-imag_part, real_part], axis=1)
    return jnp.concatenate([upper_half, lower_half], axis=0)


def row_block(matrix_rows):
    matrix_order = matrix_rows.shape[1] // 2
    return block_matrix(matrix_rows[:, :matrix_order], matrix_rows[:, matrix_order:])


def operator_matrix(elementals_wide, derivative_dirs):
    gamma_real, gamma_imag = gamma_tables()
    select = (derivative_dirs[:, None] == jnp.arange(3, dtype=jnp.int32)[None, :]).astype(
        jnp.float32
    )
    mixed_real = jnp.einsum(
        "km,kpq->mpq", select, jnp.asarray(gamma_real), precision=lax.Precision.HIGHEST
    )
    mixed_imag = jnp.einsum(
        "km,kpq->mpq", select, jnp.asarray(gamma_imag), precision=lax.Precision.HIGHEST
    )
    elem_real = elementals_wide[:, :, 0, :]
    elem_imag = elementals_wide[:, :, 1, :]
    pattern = "mpq,amb->paqb"
    real_part = jnp.einsum(
        pattern, mixed_real, elem_real, precision=lax.Precision.HIGHEST
    ) - jnp.einsum(pattern, mixed_imag, elem_imag, precision=lax.Precision.HIGHEST)
    imag_part = jnp.einsum(
        pattern, mixed_real, elem_imag, precision=lax.Precision.HIGHEST
    ) + jnp.einsum(pattern, mixed_imag, elem_real, precision=lax.Precision.HIGHEST)
    matrix_order = 4 * elementals_wide.shape[0]
    real_part = real_part.reshape((matrix_order, matrix_order)).astype(jnp.bfloat16)
    imag_part = imag_part.reshape((matrix_order, matrix_order)).astype(jnp.bfloat16)
    return block_matrix(real_part, imag_part)


def row_trace(product, first_row):
    row_count, width = product.shape
    matrix_order = width // 2
    diagonal = (
        jnp.arange(matrix_order, dtype=jnp.int32)[None, :]
        == first_row + jnp.arange(row_count, dtype=jnp.int32)[:, None]
    ).astype(jnp.float32)
    return jnp.stack(
        [
            jnp.sum(product[:, :matrix_order] * diagonal),
            jnp.sum(product[:, matrix_order:] * diagonal),
        ]
    )


def correlate(traces, source_times, insert_offsets):
    slot_count = traces.shape[0]
    counts = jnp.sum(
        (insert_offsets[:, None] == jnp.arange(3, dtype=jnp.int32)[None, :]).astype(jnp.float32),
        axis=0,
    )
    weighted = jnp.sum(traces * counts[None, :, None], axis=1)
    picker = (source_times[:, None] == jnp.arange(slot_count, dtype=jnp.int32)[None, :]).astype(
        jnp.float32
    )
    return jnp.dot(picker, weighted, precision=lax.Precision.HIGHEST)


def on_device(
    eigenvectors, gauge_links, perambulators, source_times, insert_offsets, derivative_dirs
):
    vectors = eigenvectors[0]
    link_block = gauge_links[0]
    peram_rows = perambulators[0]
    planes, side_cells, mode_count = (vectors.shape[2], vectors.shape[3], vectors.shape[5])
    spin_count = lax.axis_size("spin")
    space_count = lax.axis_size("space")
    half_modes = mode_count // spin_count
    chosen = lax.dynamic_slice_in_dim(vectors, lax.axis_index("spin") * half_modes, half_modes, 5)
    chosen_wide = chosen.astype(jnp.float32)
    norm_scale = 1.0 / math.sqrt(24.0 * planes * space_count * side_cells * side_cells)
    upper_plane = shifted(chosen[:, :, :1], "space", -1)
    columns = []
    for direction in range(3):
        spatial_axis = 4 - direction
        link_field = (
            link_block[direction]
            .reshape((2, 3, 3, planes, side_cells, side_cells))
            .astype(jnp.float32)
        )
        adjoint = times_adjoint(link_field, chosen_wide).astype(jnp.bfloat16)
        if direction == 2:
            forward_field = jnp.concatenate([chosen[:, :, 1:], upper_plane], axis=2).astype(
                jnp.float32
            )
            lower_plane = shifted(adjoint[:, :, planes - 1 :], "space", 1)
            behind = jnp.concatenate([lower_plane, adjoint[:, :, : planes - 1]], axis=2)
        else:
            forward_field = jnp.roll(chosen_wide, -1, axis=spatial_axis)
            behind = jnp.roll(adjoint, 1, axis=spatial_axis)
        behind_wide = lax.optimization_barrier(behind).astype(jnp.float32)
        derived = (times_links(link_field, forward_field) - behind_wide).astype(jnp.bfloat16)
        columns.append(derived.reshape((-1, half_modes)))
        columns.append(jnp.concatenate([derived[1], -derived[0]], axis=0).reshape((-1, half_modes)))
    stacked = jnp.stack(columns, axis=1).reshape((columns[0].shape[0], -1))
    flat_vectors = vectors.reshape((-1, mode_count))
    partial_sum = lax.dot_general(
        flat_vectors, stacked, (((0,), (0,)), ((), ())), preferred_element_type=jnp.float32
    )
    partial_sum = (partial_sum * norm_scale).reshape((mode_count, 3, 2, half_modes))
    summed = lax.psum(partial_sum, "space")
    share_rows = mode_count // space_count
    elementals = lax.dynamic_slice_in_dim(
        summed, lax.axis_index("space") * share_rows, share_rows, 0
    )
    full_rounded = lax.all_gather(summed.astype(jnp.bfloat16), "spin", axis=3, tiled=True)
    operator = operator_matrix(full_rounded.astype(jnp.float32), derivative_dirs)
    matrix_order = peram_rows.shape[1] // 2
    row_count = peram_rows.shape[0]
    first_row = lax.axis_index(("space", "spin")) * row_count
    first_product = jnp.dot(peram_rows, operator, preferred_element_type=jnp.float32) * (
        1.0 / math.sqrt(matrix_order)
    )
    first_rounded = first_product.astype(jnp.bfloat16)
    next_rows = shifted(first_rounded, "tm", -1)
    gathered = lax.all_gather(first_rounded, ("space", "spin"), axis=0, tiled=True)
    right_block = row_block(gathered)
    second_product = jnp.dot(next_rows, right_block, preferred_element_type=jnp.float32)
    second_rounded = second_product.astype(jnp.bfloat16)
    next_products = shifted(second_rounded, "tm", -1)
    third_product = jnp.dot(next_products, right_block, preferred_element_type=jnp.float32)
    local_traces = jnp.stack(
        [
            row_trace(first_product, first_row),
            row_trace(second_product, first_row),
            row_trace(third_product, first_row),
        ]
    )
    slot_count = lax.axis_size("tm")
    placed = (jnp.arange(slot_count, dtype=jnp.int32) == lax.axis_index("tm")).astype(jnp.float32)
    traces = lax.psum(placed[:, None, None] * local_traces[None], ("tm", "space", "spin"))
    correlator = correlate(traces, source_times, insert_offsets)
    chain_products = (third_product * math.sqrt(matrix_order)).astype(jnp.bfloat16)
    return (elementals[None], chain_products[None], correlator)


def solution(mesh):
    in_specs = (
        P(("cfg", "tm"), None, None, "space", None, None, None),
        P(("cfg", "tm"), None, None, None, None, "space", None),
        P(("cfg", "tm"), ("space", "spin"), None),
        P(),
        P(),
        P(),
    )
    out_specs = (
        P(("cfg", "tm"), "space", None, None, "spin"),
        P(("cfg", "tm"), ("space", "spin"), None),
        P("cfg", None),
    )
    return jax.shard_map(
        on_device, mesh=mesh, in_specs=in_specs, out_specs=out_specs, check_vma=False
    )
```

profile of v0, /device:TPU:0, one launch (start us, length us, event | category | flops | bytes accessed | tf_op | source)
XLA Modules:
  0.0 128.6 jit_solution(14775452391624116234)
XLA Ops:
  7.2 0.9 constant_dynamic-slice_fusion
  8.2 0.8 slice_convert_fusion.1
  9.0 0.3 multiply_reduce_fusion.3
  9.4 3.0 %collective-permute-start.1 = (bf16[2,3,1,2,2,64]{5,2,4,3,1,0:T(2,128)(2,1)S(1)}, bf16[2,3,1,2,2,64]{5,2,4,3,1,0:T(2,128)(2,1)S(1)}, u32[]{:S(2)}, u32[]{:S(2)}) collective-permute-start(bf16[2,3,1,2,2,64]{5,2,4,3,1,0:T(2,128)(2,1)S(1)} %pad_maximum_fusion.8), channel_id=1, source_target_pairs={{2,0},{0,2},{3,1},{1,3},{6,4},{4,6},{7,5},{5,7},{10,8},{8,10},{11,... | collective-permute-start | bytes 9224 | tf_op jit(solution)/shard_map/ppermute | solution.py:13
  13.6 0.6 collective-permute-done.1
  14.2 2.1 %collective-permute-done = bf16[2,3,1,2,2,64]{5,2,4,3,1,0:T(2,128)(2,1)S(1)} collective-permute-done((bf16[2,3,1,2,2,64]{5,2,4,3,1,0:T(2,128)(2,1)S(1)}, bf16[2,3,1,2,2,64]{5,2,4,3,1,0:T(2,128)(2,1)S(1)}, u32[]{:S(2)}, u32[]{:S(2)}) %collective-permute-start) | collective-permute-done | bytes 3104 | tf_op jit(solution)/shard_map/ppermute | solution.py:13
  17.1 0.9 convolution_multiply_fusion
  18.2 0.2 convolution_bitcast_fusion
  18.4 22.4 %all-reduce.2.cloned.1.call-done = f32[128,3,2,64]{0,3,2,1:T(8,128)} async-done(((f32[128,3,2,64]{0,3,2,1:T(8,128)}), f32[128,3,2,64]{0,3,2,1:T(8,128)}) %all-reduce.2.cloned.1.call-update) | async-done | bytes 196624 | tf_op jit(solution)/shard_map/psum | solution.py:155
  40.8 0.9 convert_element_type.105
  41.9 1.9 %all_gather.6 = bf16[128,3,2,128]{0,2,1,3:T(2,128)(2,1)S(1)} all-gather(bf16[128,3,2,64]{0,2,1,3:T(2,128)(2,1)S(1)} %copy.186), channel_id=1, replica_groups=mesh['cfg'=2,'tm'=4,'space'=2,'spin'=2] {'spin'}, dimensions={3}, use_global_device_ids=true | all-gather | bytes 294912 | tf_op jit(solution)/shard_map/all_gather | solution.py:160
  43.9 0.3 fusion.67
  44.4 0.9 fusion.27
  45.4 1.0 fusion.10
  46.8 0.9 fusion.25
  47.7 1.0 fusion.11
  49.1 1.5 %fusion.73 = (bf16[128,1024]{0,1:T(8,128)(2,1)}, f32[128,1024]{0,1:T(8,128)S(1)}) fusion(bf16[1,128,1024]{2,1,0:T(8,128)(2,1)S(1)} %copy-done, bf16[512,512]{1,0:T(8,128)(2,1)S(1)} %bitcast.176, bf16[512,512]{1,0:T(8,128)(2,1)S(1)} %fusion.64, bf16[512,512]{1,0:T(8,128)(2,1)S(1)} %bitcast.175), kind=kOutput, calls=%fused_computation.181 | convolution fusion | flops 277086208 | bytes 2621440 | tf_op jit(solution)/shard_map/dot_general | solution.py:165
  50.7 3.3 %collective-permute-start.2 = (bf16[128,1024]{0,1:T(8,128)(2,1)}, bf16[128,1024]{0,1:T(8,128)(2,1)S(1)}, u32[]{:S(2)}, u32[]{:S(2)}) collective-permute-start(bf16[128,1024]{0,1:T(8,128)(2,1)} %get-tuple-element.106), channel_id=1, source_target_pairs={{4,0},{8,4},{12,8},{0,12},{5,1},{9,5},{13,9},{1,13},{6,2},{10,6},{... | collective-permute-start | bytes 786440 | tf_op jit(solution)/shard_map/ppermute | solution.py:13
  54.0 13.5 %all-gather.2.cloned.1.call-done = bf16[512,1024]{0,1:T(8,128)(2,1)} async-done(((bf16[128,1024]{0,1:T(8,128)(2,1)}), bf16[512,1024]{0,1:T(8,128)(2,1)}) %all-gather.2.cloned.1.call-update) | async-done | bytes 1048592 | tf_op jit(solution)/shard_map/all_gather | solution.py:170
  67.5 1.4 %slice_negate_fusion = (bf16[512,512]{0,1:T(8,128)(2,1)S(1)}, bf16[512,512]{0,1:T(8,128)(2,1)S(1)}) fusion(bf16[512,1024]{0,1:T(8,128)(2,1)} %all-gather.2.cloned.1.call-done), kind=kLoop, calls=%fused_computation.24 | loop fusion | flops 262144 | bytes 2097152 | tf_op jit(solution)/shard_map/neg | solution.py:50
  69.1 1.5 %fusion.74 = (bf16[128,1024]{1,0:T(8,128)(2,1)}, f32[128,1024]{1,0:T(8,128)S(1)}) fusion(bf16[128,1024]{0,1:T(8,128)(2,1)S(1)} %collective-permute-done.2, bf16[512,512]{0,1:T(8,128)(2,1)S(1)} %get-tuple-element.64, bf16[512,512]{0,1:T(8,128)(2,1)S(1)} %get-tuple-element.63, bf16[512,1024]{0,1:T(8,128)(2,1)S(1)} %copy-done.1), kind=kOutput, calls=%fused_computation.182 | convolution fusion | flops 274857984 | bytes 3145728 | tf_op jit(solution)/shard_map/dot_general | solution.py:172
  70.6 3.3 %collective-permute-start.3 = (bf16[128,1024]{1,0:T(8,128)(2,1)}, bf16[128,1024]{1,0:T(8,128)(2,1)}, u32[]{:S(2)}, u32[]{:S(2)}) collective-permute-start(bf16[128,1024]{1,0:T(8,128)(2,1)} %get-tuple-element.108), channel_id=1, source_target_pairs={{4,0},{8,4},{12,8},{0,12},{5,1},{9,5},{13,9},{1,13},{6,2},{10,6},{... | collective-permute-start | bytes 786440 | tf_op jit(solution)/shard_map/ppermute | solution.py:13
  74.0 0.8 copy.199
  75.1 5.1 %collective-permute-done.3 = bf16[128,1024]{1,0:T(8,128)(2,1)} collective-permute-done((bf16[128,1024]{1,0:T(8,128)(2,1)}, bf16[128,1024]{1,0:T(8,128)(2,1)}, u32[]{:S(2)}, u32[]{:S(2)}) %collective-permute-start.3) | collective-permute-done | bytes 262176 | tf_op jit(solution)/shard_map/ppermute | solution.py:13
  80.2 1.9 %fusion.18 = f32[128,1024]{1,0:T(8,128)S(1)} fusion(bf16[128,1024]{1,0:T(8,128)(2,1)} %collective-permute-done.3, bf16[512,512]{0,1:T(8,128)(2,1)} %copy-done.3, bf16[512,512]{0,1:T(8,128)(2,1)S(1)} %get-tuple-element.63, bf16[512,1024]{0,1:T(8,128)(2,1)S(1)} %copy-done.1), kind=kOutput, calls=%fused_computation.20 | convolution fusion | flops 274726912 | bytes 2883584 | tf_op jit(solution)/shard_map/dot_general | solution.py:175
  82.5 0.9 fusion.22
  83.3 1.4 %maximum_bitcast_fusion = f32[1,2]{1,0:T(1,128)S(1)} fusion(f32[1]{0:T(128)} %bitcast.78, f32[1]{0:T(128)} %bitcast.77), kind=kLoop, calls=%fused_computation.163 | loop fusion | flops 2 | bytes 16 | tf_op jit(solution)/shard_map/stack | solution.py:176
  84.7 1.3 %maximum_bitcast_fusion.1 = f32[1,2]{1,0:T(1,128)S(1)} fusion(f32[1]{0:T(128)} %bitcast.81, f32[1]{0:T(128)} %bitcast.80), kind=kLoop, calls=%fused_computation.164 | loop fusion | flops 2 | bytes 16 | tf_op jit(solution)/shard_map/stack | solution.py:176
  86.0 1.3 %maximum_bitcast_fusion.2 = f32[1,2]{1,0:T(1,128)S(1)} fusion(f32[1]{0:T(128)} %bitcast.84, f32[1]{0:T(128)} %bitcast.83), kind=kLoop, calls=%fused_computation.165 | loop fusion | flops 2 | bytes 16 | tf_op jit(solution)/shard_map/stack | solution.py:176
  87.4 0.8 fusion.20
  88.2 32.7 %psum.15 = f32[4,3,2]{0,2,1:T(2,128)S(1)} all-reduce(f32[4,3,2]{0,2,1:T(2,128)S(1)} %broadcast_multiply_fusion), channel_id=1, replica_groups=mesh['cfg'=2,'tm'=4,'space'=2,'spin'=2] {'tm','space','spin'}, use_global_device_ids=true, to_apply=%region_31.32 | all-reduce | flops 24 | bytes 192 | tf_op jit(solution)/shard_map/psum | solution.py:185
  121.0 0.8 fusion.53
  (102 shorter events, 4.1 us)
Async XLA Ops:
  7.2 41.9 %copy-start = (bf16[1,128,1024]{2,1,0:T(8,128)(2,1)S(1)}, bf16[1,128,1024]{2,1,0:T(8,128)(2,1)}, u32[]{:S(2)}) copy-start(bf16[1,128,1024]{2,1,0:T(8,128)(2,1)} %param.10) | copy-start | bytes 786436
  7.2 33.7 %all-reduce.2.cloned.1.call-start = ((), (), s32[]{:S(2)}) async-start(), calls=%async_computation | async-start | bytes 393216 | tf_op jit(solution)/shard_map/psum | solution.py:155
  9.4 4.7 %collective-permute-start.1 = (bf16[2,3,1,2,2,64]{5,2,4,3,1,0:T(2,128)(2,1)S(1)}, bf16[2,3,1,2,2,64]{5,2,4,3,1,0:T(2,128)(2,1)S(1)}, u32[]{:S(2)}, u32[]{:S(2)}) collective-permute-start(bf16[2,3,1,2,2,64]{5,2,4,3,1,0:T(2,128)(2,1)S(1)} %pad_maximum_fusion.8), channel_id=1, source_target_pairs={{2,0},{0,2},{3,1},{1,3},{6,4},{4,6},{7,5},{5,7},{10,8},{8,10},{11,... | collective-permute-start | bytes 9224 | tf_op jit(solution)/shard_map/ppermute | solution.py:13
  12.5 3.8 %collective-permute-start = (bf16[2,3,1,2,2,64]{5,2,4,3,1,0:T(2,128)(2,1)S(1)}, bf16[2,3,1,2,2,64]{5,2,4,3,1,0:T(2,128)(2,1)S(1)}, u32[]{:S(2)}, u32[]{:S(2)}) collective-permute-start(bf16[2,3,1,2,2,64]{5,2,4,3,1,0:T(2,128)(2,1)S(1)} %slice.278), channel_id=1, source_target_pairs={{2,0},{0,2},{3,1},{1,3},{6,4},{4,6},{7,5},{5,7},{10,8},{8,10},{11,... | collective-permute-start | bytes 9224 | tf_op jit(solution)/shard_map/ppermute | solution.py:13
  16.3 0.8 copy-start.4
  16.5 1.6 %copy-start.6 = (f32[3,4,4]{2,0,1:T(4,128)S(1)}, f32[3,4,4]{2,0,1:T(4,128)}, u32[]{:S(2)}) copy-start(f32[3,4,4]{2,0,1:T(4,128)} %constant.38.clone) | copy-start | bytes 580
  16.5 1.6 %copy-start.7 = (s32[3]{0:T(128)S(1)}, s32[3]{0:T(128)}, u32[]{:S(2)}) copy-start(s32[3]{0:T(128)} %param.13) | copy-start | bytes 40
  16.5 1.7 %copy-start.5 = (f32[3,4,4]{2,0,1:T(4,128)S(1)}, f32[3,4,4]{2,0,1:T(4,128)}, u32[]{:S(2)}) copy-start(f32[3,4,4]{2,0,1:T(4,128)} %constant.39.clone) | copy-start | bytes 580
  18.0 49.5 %all-gather.2.cloned.1.call-start = ((), (), s32[]{:S(2)}) async-start(), calls=%async_computation.1 | async-start | bytes 1310720 | tf_op jit(solution)/shard_map/all_gather | solution.py:170
  49.1 1.5 %copy-start.8 = (s32[4]{0:T(128)S(1)}, s32[4]{0:T(128)}, u32[]{:S(2)}) copy-start(s32[4]{0:T(128)} %param.12) | copy-start | bytes 52
  50.7 18.2 %collective-permute-start.2 = (bf16[128,1024]{0,1:T(8,128)(2,1)}, bf16[128,1024]{0,1:T(8,128)(2,1)S(1)}, u32[]{:S(2)}, u32[]{:S(2)}) collective-permute-start(bf16[128,1024]{0,1:T(8,128)(2,1)} %get-tuple-element.106), channel_id=1, source_target_pairs={{4,0},{8,4},{12,8},{0,12},{5,1},{9,5},{13,9},{1,13},{6,2},{10,6},{... | collective-permute-start | bytes 786440 | tf_op jit(solution)/shard_map/ppermute | solution.py:13
  67.5 1.5 %copy-start.1 = (bf16[512,1024]{0,1:T(8,128)(2,1)S(1)}, bf16[512,1024]{0,1:T(8,128)(2,1)}, u32[]{:S(2)}) copy-start(bf16[512,1024]{0,1:T(8,128)(2,1)} %all-gather.2.cloned.1.call-done) | copy-start | bytes 3145732
  68.9 1.7 %copy-start.3 = (bf16[512,512]{0,1:T(8,128)(2,1)}, bf16[512,512]{0,1:T(8,128)(2,1)S(1)}, u32[]{:S(2)}) copy-start(bf16[512,512]{0,1:T(8,128)(2,1)S(1)} %get-tuple-element.64) | copy-start | bytes 1572868
  69.1 4.9 %copy-start.2 = (f32[128,3,2,64]{0,3,2,1:T(8,128)S(1)}, f32[128,3,2,64]{0,3,2,1:T(8,128)}, u32[]{:S(2)}) copy-start(f32[128,3,2,64]{0,3,2,1:T(8,128)} %all-reduce.2.cloned.1.call-done) | copy-start | bytes 589828
  70.6 9.6 %collective-permute-start.3 = (bf16[128,1024]{1,0:T(8,128)(2,1)}, bf16[128,1024]{1,0:T(8,128)(2,1)}, u32[]{:S(2)}, u32[]{:S(2)}) collective-permute-start(bf16[128,1024]{1,0:T(8,128)(2,1)} %get-tuple-element.108), channel_id=1, source_target_pairs={{4,0},{8,4},{12,8},{0,12},{5,1},{9,5},{13,9},{1,13},{6,2},{10,6},{... | collective-permute-start | bytes 786440 | tf_op jit(solution)/shard_map/ppermute | solution.py:13
  82.5 38.6 %copy-start.9 = (s32[16]{0:T(128)S(1)}, s32[16]{0:T(128)}, u32[]{:S(2)}) copy-start(s32[16]{0:T(128)} %param.11) | copy-start | bytes 196
Sparse Core Ops, SparseCore 0:
  18.1 22.7 all-reduce.1
  50.7 16.8 all-gather.1
where the time goes:
time: 129 us
  waiting for transfers between devices  43.6 us (34%)
  blocking collectives  34.7 us (27%)
  between operations  14.8 us (11%)
  matrix products  10.9 us (8%)
  other arithmetic  10.2 us (8%)
  starting transfers between devices  9.86 us (8%)
  local copies, waits for them, and re-layouts  4.58 us (4%)
    psum x1, blocking collectives, on_device(): lax.psum(placed[:, None, None] * local_traces[None], ('tm', 'space', 'spi...  32.7 us
    psum x1, waiting for transfers between devices, on_device(): summed = lax.psum(partial_sum, 'space')  22.4 us
    all_gather x1, waiting for transfers between devices, on_device(): lax.all_gather(first_rounded, ('space', 'spin'), axis=0, tiled=True)  13.5 us
    ppermute x4, starting transfers between devices, shifted(): return lax.ppermute(block, axis, route)  9.78 us
    ppermute x4, waiting for transfers between devices, shifted(): return lax.ppermute(block, axis, route)  7.69 us
    another operation x4, other arithmetic, on_device(): jnp.stack([row_trace(first_product, first_row), row_trace(second_product,...  4.04 us
  transfers between devices with their start and end apart: 6, of which 5 were waited for; matrix products, arithmetic and copies ran while one was open for 3% of the time, Pallas kernels for 0%

commit v1 on v0

v1 whole, which is shorter than its diff:
```python
import functools
import math

import jax
import jax.numpy as jnp
import numpy as np
from jax import lax
from jax.experimental import pallas as pl
from jax.experimental.pallas import tpu as pltpu
from jax.sharding import PartitionSpec as P

MESH = pl.DeviceIdType.MESH
F32 = jnp.float32
BF16 = jnp.bfloat16
CHUNKS = 2


def dot(a, b, dims=(((1,), (0,)), ((), ()))):
    return lax.dot_general(a, b, dims, preferred_element_type=F32)


def shift_table(depth, side):
    site = np.arange(depth * side * side)
    z, y, x = site // (side * side), (site // side) % side, site % side
    targets = [
        (z * side + y) * side + (x + 1) % side,
        (z * side + (y + 1) % side) * side + x,
        (((z + 1) % depth) * side + y) * side + x,
    ]
    table = np.zeros((3 * site.size, site.size), np.float32)
    for direction, target in enumerate(targets):
        table[direction * site.size + site, target] = 1.0
    return table


def diagonal_sums(product, first_row):
    rows, width = product.shape
    order = width // 2
    hit = lax.broadcasted_iota(jnp.int32, (rows, order), 1) == (
        first_row + lax.broadcasted_iota(jnp.int32, (rows, order), 0)
    )
    return (
        jnp.sum(jnp.where(hit, product[:, :order], 0.0)),
        jnp.sum(jnp.where(hit, product[:, order:], 0.0)),
    )


def complex_rows(left, right):
    rows, width = left.shape
    order = width // 2
    both = dot(jnp.concatenate([left[:, :order], left[:, order:]], axis=0), right)
    top, bottom = both[:rows], both[rows:]
    return jnp.concatenate(
        [top[:, :order] - bottom[:, order:], top[:, order:] + bottom[:, :order]], axis=1
    )


def first_rows(peram, mixed):
    rows, width = peram.shape
    order = width // 2
    half = order // 2
    stacked = jnp.concatenate(
        [
            peram[:, half:order],
            peram[:, order + half :],
            peram[:, :half],
            peram[:, order : order + half],
        ],
        axis=0,
    )
    y = dot(stacked, mixed)
    down_real = y[:rows, :half] - y[rows : 2 * rows, half:]
    down_imag = y[:rows, half:] + y[rows : 2 * rows, :half]
    up_real = y[2 * rows : 3 * rows, :half] - y[3 * rows :, half:]
    up_imag = y[2 * rows : 3 * rows, half:] + y[3 * rows :, :half]
    return jnp.concatenate([-down_imag, up_imag, down_real, -up_real], axis=1) * (
        1.0 / math.sqrt(order)
    )


def kernel(
    sizes,
    v_ref,
    l_ref,
    p_ref,
    table_ref,
    src_ref,
    off_ref,
    dirs_ref,
    elem_ref,
    chain_ref,
    corr_ref,
    v_all,
    l_all,
    p_all,
    e_all,
    m_ref,
    f_all,
    f_next,
    s_own,
    s_next,
    t_all,
    v_send,
    v_recv,
    l_send,
    l_recv,
    p_send,
    p_recv,
    q_send,
    q_recv,
    z_send,
    z_recv,
    t_send,
    t_recv,
):
    T, S, K = sizes
    G = S * K
    t, s, k = lax.axis_index("tm"), lax.axis_index("space"), lax.axis_index("spin")
    rank = s * K + k
    rows = p_ref.shape[0]
    order = p_ref.shape[1] // 2
    modes = v_ref.shape[2]
    first_row = rank * rows
    mine = pl.ds(pl.multiple_of(first_row, rows), rows)
    below, above = lax.rem(t + T - 1, T), lax.rem(t + 1, T)

    barrier = pltpu.get_barrier_semaphore()
    for j in range(1, G):
        other = lax.rem(rank + j, G)
        pl.semaphore_signal(
            barrier,
            inc=1,
            device_id={"tm": t, "space": lax.div(other, K), "spin": lax.rem(other, K)},
            device_id_type=MESH,
        )
    for target in (below, above):
        pl.semaphore_signal(barrier, inc=1, device_id={"tm": target}, device_id_type=MESH)
    pl.semaphore_wait(barrier, G + 1)

    sends = []
    for j in range(1, S):
        other = lax.rem(s + j, S)
        for source, target, send_sem, recv_sem in (
            (v_ref, v_all.at[s], v_send, v_recv),
            (l_ref, l_all.at[s], l_send, l_recv),
        ):
            copy = pltpu.make_async_remote_copy(
                source, target, send_sem.at[j], recv_sem.at[s],
                device_id={"space": other}, device_id_type=MESH,
            )
            copy.start()
            sends.append(copy)
    for j in range(1, S):
        other = lax.rem(s + j, S)
        copy = pltpu.make_async_remote_copy(
            p_ref, p_all.at[mine], p_send.at[j], p_recv.at[s],
            device_id={"space": other}, device_id_type=MESH,
        )
        copy.start()
        sends.append(copy)
    for i in range(1, K):
        copy = pltpu.make_async_remote_copy(
            p_ref, p_all.at[mine], q_send.at[0, i], q_recv.at[rank],
            device_id={"spin": lax.rem(k + i, K)}, device_id_type=MESH,
        )
        copy.start()
        sends.append(copy)
    v_all[s] = v_ref[...]
    l_all[s] = l_ref[...]

    for j in range(1, S):
        other = lax.rem(s + j, S)
        for ref, sem in ((v_all, v_recv), (l_all, l_recv)):
            pltpu.make_async_copy(ref.at[other], ref.at[other], sem.at[other]).wait()

    slab = v_ref.shape[1]
    sites = S * slab
    fields = [jnp.concatenate([v_all[i, j] for i in range(S)], axis=0) for j in range(6)]
    moved = dot(table_ref[...], jnp.concatenate(fields, axis=1))
    eye = (
        lax.broadcasted_iota(jnp.int32, (slab, slab), 0)
        == lax.broadcasted_iota(jnp.int32, (slab, slab), 1)
    ).astype(F32).astype(BF16)
    links = jnp.concatenate(
        [dot(eye, l_all[i], (((1,), (1,)), ((), ()))) for i in range(S)], axis=0
    )
    columns = []
    for mu in range(3):
        ahead = [
            moved[mu * sites : (mu + 1) * sites, j * modes : (j + 1) * modes] for j in range(6)
        ]
        real_rows, imag_rows = [], []
        for c in range(3):
            real, imag = None, None
            for d in range(3):
                at = (mu * 6 + c) * 3 + d
                u_real = links[:, at : at + 1]
                u_imag = links[:, at + 9 : at + 10]
                more_real = u_real * ahead[d] - u_imag * ahead[3 + d]
                more_imag = u_real * ahead[3 + d] + u_imag * ahead[d]
                real = more_real if real is None else real + more_real
                imag = more_imag if imag is None else imag + more_imag
            real_rows.append(real.astype(BF16))
            imag_rows.append(imag.astype(BF16))
        columns.append(jnp.concatenate(real_rows + imag_rows, axis=0))
        columns.append(jnp.concatenate(imag_rows + [-r for r in real_rows], axis=0))
    norm_scale = 1.0 / math.sqrt(24.0 * sites)
    product = dot(
        jnp.concatenate(fields, axis=0), jnp.concatenate(columns, axis=1), (((0,), (0,)), ((), ()))
    ) * norm_scale
    for mu in range(3):
        a_real = product[:, (2 * mu) * modes : (2 * mu + 1) * modes]
        a_imag = product[:, (2 * mu + 1) * modes : (2 * mu + 2) * modes]
        e_all[mu, 0] = a_real - a_real.T
        e_all[mu, 1] = a_imag + a_imag.T

    def picked(gamma, part):
        return e_all[dirs_ref[gamma], part].astype(BF16).astype(F32)

    e0r, e0i, e1r, e1i, e2r, e2i = [picked(g, part) for g in range(3) for part in range(2)]
    m_ref[...] = jnp.concatenate(
        [
            jnp.concatenate([e2r, e0r + e1i, e2i, e0i - e1r], axis=1),
            jnp.concatenate([e0r - e1i, -e2r, e0i + e1r, -e2i], axis=1),
        ],
        axis=0,
    ).astype(BF16)

    part = rows // CHUNKS
    diagonals = []

    def to_below(source, target, index):
        copy = pltpu.make_async_remote_copy(
            source, target, z_send.at[index], z_recv.at[index],
            device_id={"tm": below}, device_id_type=MESH,
        )
        copy.start()
        return copy

    z_copies = []
    real_sum, imag_sum = 0.0, 0.0
    for i in range(CHUNKS):
        wide = first_rows(p_ref[i * part : (i + 1) * part, :], m_ref[...])
        span = pl.ds(pl.multiple_of(first_row + i * part, part), part)
        f_all[span, :] = wide.astype(BF16)
        z_copies.append(to_below(f_all.at[span], f_next.at[pl.ds(i * part, part)], i))
        more_real, more_imag = diagonal_sums(wide, first_row + i * part)
        real_sum, imag_sum = real_sum + more_real, imag_sum + more_imag
    diagonals += [real_sum, imag_sum]

    for j in range(1, S):
        other = lax.rem(s + j, S)
        block = pl.ds(pl.multiple_of((other * K + k) * rows, rows), rows)
        pltpu.make_async_copy(p_all.at[block], p_all.at[block], p_recv.at[other]).wait()
        for i in range(1, K):
            copy = pltpu.make_async_remote_copy(
                p_all.at[block], p_all.at[block], q_send.at[j, i], q_recv.at[other * K + k],
                device_id={"spin": lax.rem(k + i, K)}, device_id_type=MESH,
            )
            copy.start()
            sends.append(copy)
        f_all[block, :] = first_rows(p_all[block, :], m_ref[...]).astype(BF16)
    for j in range(S):
        for i in range(1, K):
            owner = lax.rem(s + j, S) * K + lax.rem(k + i, K)
            block = pl.ds(pl.multiple_of(owner * rows, rows), rows)
            pltpu.make_async_copy(p_all.at[block], p_all.at[block], q_recv.at[owner]).wait()
            f_all[block, :] = first_rows(p_all[block, :], m_ref[...]).astype(BF16)

    share, half = elem_ref.shape[0], elem_ref.shape[3]
    own_rows = pl.ds(pl.multiple_of(s * share, share), share)
    for mu in range(3):
        for ri in range(2):
            block = e_all[mu, ri, own_rows, :]
            mine_columns = block[:, :half]
            for i in range(1, K):
                mine_columns = jnp.where(k == i, block[:, i * half : (i + 1) * half], mine_columns)
            elem_ref[:, mu, ri, :] = mine_columns

    real_sum, imag_sum = 0.0, 0.0
    for i in range(CHUNKS):
        span = pl.ds(i * part, part)
        z_copies[i].wait_recv()
        wide = complex_rows(f_next[span, :], f_all[...])
        s_own[span, :] = wide.astype(BF16)
        z_copies.append(to_below(s_own.at[span], s_next.at[span], CHUNKS + i))
        more_real, more_imag = diagonal_sums(wide, first_row + i * part)
        real_sum, imag_sum = real_sum + more_real, imag_sum + more_imag
    diagonals += [real_sum, imag_sum]

    real_sum, imag_sum = 0.0, 0.0
    for i in range(CHUNKS):
        span = pl.ds(i * part, part)
        z_copies[CHUNKS + i].wait_recv()
        wide = complex_rows(s_next[span, :], f_all[...])
        chain_ref[span, :] = (wide * math.sqrt(order)).astype(BF16)
        more_real, more_imag = diagonal_sums(wide, first_row + i * part)
        real_sum, imag_sum = real_sum + more_real, imag_sum + more_imag
    diagonals += [real_sum, imag_sum]

    tile_row = lax.broadcasted_iota(jnp.int32, (8, 128), 0)
    tile_lane = lax.broadcasted_iota(jnp.int32, (8, 128), 1)
    tile = jnp.zeros((8, 128), F32)
    for o in range(3):
        for ri in range(2):
            tile = jnp.where((tile_row == o) & (tile_lane == ri), diagonals[2 * o + ri], tile)
    total = T * G
    me = t * G + rank
    t_all[me] = tile

    def trace_copy(j):
        other = lax.rem(me + j, total)
        group = lax.rem(other, G)
        return other, pltpu.make_async_remote_copy(
            t_all.at[me], t_all.at[me], t_send.at[j], t_recv.at[me],
            device_id={
                "tm": lax.div(other, G), "space": lax.div(group, K), "spin": lax.rem(group, K)
            },
            device_id_type=MESH,
        )

    def start_trace(j, carry):
        trace_copy(j)[1].start()
        return carry

    lax.fori_loop(1, total, start_trace, 0)

    def wait_trace(j, carry):
        other, copy = trace_copy(j)
        copy.wait_send()
        pltpu.make_async_copy(t_all.at[other], t_all.at[other], t_recv.at[other]).wait()
        return carry

    lax.fori_loop(1, total, wait_trace, 0)

    counts = []
    for o in range(3):
        count = 0
        for j in range(off_ref.shape[0]):
            count = count + jnp.where(off_ref[j] == o, 1, 0)
        counts.append(count.astype(F32))
    weight = jnp.zeros((8, 128), F32)
    for o in range(3):
        weight = jnp.where(tile_row == o, counts[o], weight)
    sources = src_ref.shape[0]
    out_row = lax.broadcasted_iota(jnp.int32, (sources, 128), 0)
    wanted = jnp.zeros((sources, 128), jnp.int32)
    for n in range(sources):
        wanted = jnp.where(out_row == n, src_ref[n], wanted)

    def add_time(i, acc):
        summed = t_all[i * G]
        for g in range(1, G):
            summed = summed + t_all[i * G + g]
        line = jnp.sum(summed * weight, axis=0, keepdims=True)
        return acc + jnp.where(wanted == i, line, 0.0)

    found = lax.fori_loop(0, T, add_time, jnp.zeros((sources, 128), F32))
    corr_ref[...] = found[:, : corr_ref.shape[1]]

    for copy in sends:
        copy.wait_send()
    for copy in z_copies:
        copy.wait_send()


def on_device(
    sizes, eigenvectors, gauge_links, perambulators, source_times, insert_offsets, derivative_dirs
):
    T, S, K = sizes
    _, _, _, planes, side, _, modes = eigenvectors.shape
    slab = planes * side * side
    vectors = eigenvectors.reshape((6, slab, modes))
    links = gauge_links.reshape((54, slab))
    peram = perambulators[0]
    rows, width = peram.shape
    order = width // 2
    table = jnp.asarray(shift_table(planes * S, side), BF16)
    vmem = pl.BlockSpec(memory_space=pltpu.VMEM)
    smem = pl.BlockSpec(memory_space=pltpu.SMEM)
    dma = pltpu.SemaphoreType.DMA
    elementals, chain, correlator = pl.pallas_call(
        functools.partial(kernel, sizes),
        out_shape=(
            jax.ShapeDtypeStruct((modes // S, 3, 2, modes // K), F32),
            jax.ShapeDtypeStruct((rows, width), BF16),
            jax.ShapeDtypeStruct((source_times.shape[0], 2), F32),
        ),
        in_specs=[vmem, vmem, vmem, vmem, smem, smem, smem],
        out_specs=(vmem, vmem, vmem),
        scratch_shapes=[
            pltpu.VMEM((S, 6, slab, modes), BF16),
            pltpu.VMEM((S, 54, slab), BF16),
            pltpu.VMEM((order, width), BF16),
            pltpu.VMEM((3, 2, modes, modes), F32),
            pltpu.VMEM((2 * modes, 4 * modes), BF16),
            pltpu.VMEM((order, width), BF16),
            pltpu.VMEM((rows, width), BF16),
            pltpu.VMEM((rows, width), BF16),
            pltpu.VMEM((rows, width), BF16),
            pltpu.VMEM((T * S * K, 8, 128), F32),
            dma((S,)),
            dma((S,)),
            dma((S,)),
            dma((S,)),
            dma((S,)),
            dma((S,)),
            dma((S, K)),
            dma((S * K,)),
            dma((2 * CHUNKS,)),
            dma((2 * CHUNKS,)),
            dma((T * S * K,)),
            dma((T * S * K,)),
        ],
        compiler_params=pltpu.CompilerParams(collective_id=0, has_side_effects=True),
    )(vectors, links, peram, table, source_times, insert_offsets, derivative_dirs)
    return (elementals[None], chain[None], correlator)


def solution(mesh):
    sizes = (mesh.shape["tm"], mesh.shape["space"], mesh.shape["spin"])
    in_specs = (
        P(("cfg", "tm"), None, None, "space", None, None, None),
        P(("cfg", "tm"), None, None, None, None, "space", None),
        P(("cfg", "tm"), ("space", "spin"), None),
        P(),
        P(),
        P(),
    )
    out_specs = (
        P(("cfg", "tm"), "space", None, None, "spin"),
        P(("cfg", "tm"), ("space", "spin"), None),
        P("cfg", None),
    )
    return jax.shard_map(
        functools.partial(on_device, sizes),
        mesh=mesh,
        in_specs=in_specs,
        out_specs=out_specs,
        check_vma=False,
    )
```

time: 129 us -> 38.3 us (0.30)
  waiting for transfers between devices: 43.6 us -> 0 us
  blocking collectives: 34.7 us -> 0 us
  Pallas kernels: 0 us -> 31.7 us
  between operations: 14.8 us -> 0.65 us
  matrix products: 10.9 us -> 0 us
  other arithmetic: 10.2 us -> 0 us
  starting transfers between devices: 9.86 us -> 0 us
    psum x1 -> x0, blocking collectives: 32.7 us -> none  [on_device(): lax.psum(placed[:, None, None] * local_traces[None], ('tm', 'space', 'spi...]
    pallas_call x0 -> x1, Pallas kernels: none -> 31.7 us  [on_device(): pl.pallas_call(functools.partial(kernel, sizes), out_shape=(jax.ShapeDtyp...]
    psum x1 -> x0, waiting for transfers between devices: 22.4 us -> none  [on_device(): summed = lax.psum(partial_sum, 'space')]
    all_gather x1 -> x0, waiting for transfers between devices: 13.5 us -> none  [on_device(): lax.all_gather(first_rounded, ('space', 'spin'), axis=0, tiled=True)]
    dot_general x11 -> x0, matrix products: 10.9 us -> none  [the longest x1 1.93 us: on_device(): jnp.dot(next_products, right_block, preferred_element_type=jnp.float32)]
    ppermute x4 -> x0, starting transfers between devices: 9.78 us -> none  [shifted(): return lax.ppermute(block, axis, route)]
    ppermute x4 -> x0, waiting for transfers between devices: 7.69 us -> none  [shifted(): return lax.ppermute(block, axis, route)]
    another operation x6 -> x0, other arithmetic: 4.05 us -> none  [the longest x4 4.04 us: on_device(): jnp.stack([row_trace(first_product, first_row), row_trace(second_product,...]
  transfers between devices with their start and end apart: 6 -> 0, of which waited for: 5 -> 0; matrix products, arithmetic and copies ran while one was open for 3% -> 0% of each run, Pallas kernels for 0% -> 0%
where the time goes in v1:
time: 38.3 us; the launch traced here: 38.1 us
  Pallas kernels  31.7 us (83%)
  local copies, waits for them, and re-layouts  5.67 us (15%)
  between operations  0.65 us (2%)
    pallas_call x1, Pallas kernels, on_device(): pl.pallas_call(functools.partial(kernel, sizes), out_shape=(jax.ShapeDtyp...  31.7 us
    unnamed x6, local copies, waits for them, and re-layouts  4.95 us

profile of v1, /device:TPU:0, one launch (start us, length us, event | category | flops | bytes accessed | tf_op | source)
XLA Modules:
  0.0 38.1 jit_solution(9850306081510272134)
XLA Ops:
  0.6 1.2 %copy.12 = bf16[1,3,2,3,3,8,4]{6,5,4,3,2,1,0:T(8,128)(2,1)S(1)} copy(bf16[1,3,2,3,3,8,4]{5,6,4,3,2,1,0:T(4,128)(2,1)} %param.8) | data formatting | bytes 6912 | tf_op args[1]
  1.8 0.7 %reshape.13.l_ref = bf16[54,32]{1,0:T(8,128)(2,1)} reshape(bf16[1,3,2,3,3,8,4]{6,5,4,3,2,1,0:T(8,128)(2,1)S(1)} %copy.12) | data formatting | bytes 6912 | tf_op jit(solution)/shard_map/reshape | solution.py:374
  2.6 31.7 %shard_map.94 = (f32[64,3,2,64]{3,2,1,0:T(2,128)}, bf16[128,1024]{1,0:T(8,128)(2,1)}, f32[16,2]{1,0:T(8,128)}) custom-call(bf16[6,32,128]{2,1,0:T(8,128)(2,1)} %bitcast.9, bf16[54,32]{1,0:T(8,128)(2,1)} %reshape.13.l_ref, bf16[128,1024]{1,0:T(8,128)(2,1)} %bitcast.6, bf16[192,64]{1,0:T(8,128)(2,1)} %constant.2.clone.table_ref, s32[16]{0:T(128)} %src_ref.1, ...), custom_call_target="tpu_custom_call" | custom-call | tf_op jit(solution)/shard_map/pallas_call | solution.py:382
  34.3 0.0 copy-start
  34.3 1.4 %copy.13 = f32[16,2]{0,1:T(2,128)} copy(f32[16,2]{1,0:T(8,128)} %get-tuple-element.14) | data formatting | bytes 256
  35.7 1.6 %copy.16 = f32[1,64,3,2,64]{4,3,2,1,0:T(2,128)} copy(f32[1,64,3,2,64]{4,3,2,1,0:T(2,128)} %bitcast.8) | data formatting | bytes 196608
  37.4 0.0 copy-done
  37.4 0.7 %copy.17 = bf16[1,128,1024]{2,1,0:T(8,128)(2,1)} copy(bf16[1,128,1024]{2,1,0:T(8,128)(2,1)S(1)} %bitcast.7) | data formatting | bytes 524288
Async XLA Ops:
  34.3 3.0 %copy-start = (bf16[128,1024]{1,0:T(8,128)(2,1)S(1)}, bf16[128,1024]{1,0:T(8,128)(2,1)}, u32[]{:S(2)}) copy-start(bf16[128,1024]{1,0:T(8,128)(2,1)} %get-tuple-element.7) | copy-start | bytes 786436

commit v2 on v1

--- a/solution.py
+++ b/solution.py
@@ -12,37 +12,50 @@
 MESH = pl.DeviceIdType.MESH
 F32 = jnp.float32
 BF16 = jnp.bfloat16
-CHUNKS = 2
+CHUNKS = 4
 
 
 def dot(a, b, dims=(((1,), (0,)), ((), ()))):
     return lax.dot_general(a, b, dims, preferred_element_type=F32)
 
 
-def shift_table(depth, side):
-    site = np.arange(depth * side * side)
-    z, y, x = site // (side * side), (site // side) % side, site % side
+def shift_table(slabs, planes, side):
+    depth, area = slabs * planes, side * side
+    slab, cell, plane = np.meshgrid(
+        np.arange(slabs), np.arange(area), np.arange(planes), indexing="ij"
+    )
+    z, y, x = (slab * planes + plane).ravel(), (cell // side).ravel(), (cell % side).ravel()
+    count = z.size
+
+    def plain(z, y, x):
+        return ((z % depth) * side + y % side) * side + x % side
+
+    def ordered(z, y, x):
+        z = z % depth
+        return ((z // planes) * area + (y % side) * side + x % side) * planes + z % planes
+
     targets = [
-        (z * side + y) * side + (x + 1) % side,
-        (z * side + (y + 1) % side) * side + x,
-        (((z + 1) % depth) * side + y) * side + x,
+        plain(z, y, x), plain(z, y, x + 1), plain(z, y + 1, x), plain(z + 1, y, x),
+        ordered(z, y, x - 1), ordered(z, y - 1, x), ordered(z - 1, y, x),
     ]
-    table = np.zeros((3 * site.size, site.size), np.float32)
-    for direction, target in enumerate(targets):
-        table[direction * site.size + site, target] = 1.0
+    table = np.zeros((len(targets) * count, count), np.float32)
+    for block, target in enumerate(targets):
+        table[block * count + np.arange(count), target] = 1.0
     return table
 
 
-def diagonal_sums(product, first_row):
+def diagonal_lines(product, first_row, lanes=128):
     rows, width = product.shape
     order = width // 2
     hit = lax.broadcasted_iota(jnp.int32, (rows, order), 1) == (
         first_row + lax.broadcasted_iota(jnp.int32, (rows, order), 0)
     )
-    return (
-        jnp.sum(jnp.where(hit, product[:, :order], 0.0)),
-        jnp.sum(jnp.where(hit, product[:, order:], 0.0)),
-    )
+    lines = []
+    for half in (product[:, :order], product[:, order:]):
+        kept = jnp.where(hit, half, 0.0)
+        folded = sum(kept[:, i : i + lanes] for i in range(0, order, lanes))
+        lines.append(jnp.sum(folded, axis=0, keepdims=True))
+    return jnp.concatenate(lines, axis=0)
 
 
 def complex_rows(left, right):
@@ -91,6 +104,7 @@
     chain_ref,
     corr_ref,
     v_all,
+    l_own,
     l_all,
     p_all,
     e_all,
@@ -124,6 +138,13 @@
     mine = pl.ds(pl.multiple_of(first_row, rows), rows)
     below, above = lax.rem(t + T - 1, T), lax.rem(t + 1, T)
 
+    planes = l_ref.shape[1]
+    eye = (
+        lax.broadcasted_iota(jnp.int32, (planes, planes), 0)
+        == lax.broadcasted_iota(jnp.int32, (planes, planes), 1)
+    ).astype(F32).astype(BF16)
+    l_own[...] = dot(eye, l_ref[...], (((1,), (1,)), ((), ()))).astype(BF16)
+
     barrier = pltpu.get_barrier_semaphore()
     for j in range(1, G):
         other = lax.rem(rank + j, G)
@@ -142,7 +163,7 @@
         other = lax.rem(s + j, S)
         for source, target, send_sem, recv_sem in (
             (v_ref, v_all.at[s], v_send, v_recv),
-            (l_ref, l_all.at[s], l_send, l_recv),
+            (l_own, l_all.at[s], l_send, l_recv),
         ):
             copy = pltpu.make_async_remote_copy(
                 source, target, send_sem.at[j], recv_sem.at[s],
@@ -166,7 +187,7 @@
         copy.start()
         sends.append(copy)
     v_all[s] = v_ref[...]
-    l_all[s] = l_ref[...]
+    l_all[s] = l_own[...]
 
     for j in range(1, S):
         other = lax.rem(s + j, S)
@@ -175,44 +196,58 @@
 
     slab = v_ref.shape[1]
     sites = S * slab
+    cells = slab // planes
     fields = [jnp.concatenate([v_all[i, j] for i in range(S)], axis=0) for j in range(6)]
-    moved = dot(table_ref[...], jnp.concatenate(fields, axis=1))
-    eye = (
-        lax.broadcasted_iota(jnp.int32, (slab, slab), 0)
-        == lax.broadcasted_iota(jnp.int32, (slab, slab), 1)
-    ).astype(F32).astype(BF16)
-    links = jnp.concatenate(
-        [dot(eye, l_all[i], (((1,), (1,)), ((), ()))) for i in range(S)], axis=0
-    )
+    moved = dot(table_ref[: 4 * sites, :], jnp.concatenate(fields, axis=1))
+
+    def field(block, j):
+        return moved[block * sites : (block + 1) * sites, j * modes : (j + 1) * modes]
+
+    here = [field(0, j) for j in range(6)]
+    link_lines = [l_all[i].astype(F32) for i in range(S)]
+
+    def link(mu, ri, row, column):
+        first = (((mu * 2 + ri) * 3 + row) * 3 + column) * cells
+        return jnp.concatenate(
+            [
+                jnp.broadcast_to(line[:, first + cell : first + cell + 1], (planes, modes))
+                for line in link_lines
+                for cell in range(cells)
+            ],
+            axis=0,
+        )
+
     columns = []
     for mu in range(3):
-        ahead = [
-            moved[mu * sites : (mu + 1) * sites, j * modes : (j + 1) * modes] for j in range(6)
+        ahead = [field(1 + mu, j) for j in range(6)]
+        forward = [0.0] * 6
+        adjoint = [0.0] * 6
+        for row in range(3):
+            for column in range(3):
+                real, imag = link(mu, 0, row, column), link(mu, 1, row, column)
+                forward[row] += real * ahead[column] - imag * ahead[3 + column]
+                forward[3 + row] += real * ahead[3 + column] + imag * ahead[column]
+                adjoint[column] += real * here[row] + imag * here[3 + row]
+                adjoint[3 + column] += real * here[3 + row] - imag * here[row]
+        behind = dot(
+            table_ref[(4 + mu) * sites : (5 + mu) * sites, :],
+            jnp.concatenate([a.astype(BF16) for a in adjoint], axis=1),
+        )
+        derived = [
+            (forward[j] - behind[:, j * modes : (j + 1) * modes]).astype(BF16) for j in range(6)
         ]
-        real_rows, imag_rows = [], []
-        for c in range(3):
-            real, imag = None, None
-            for d in range(3):
-                at = (mu * 6 + c) * 3 + d
-                u_real = links[:, at : at + 1]
-                u_imag = links[:, at + 9 : at + 10]
-                more_real = u_real * ahead[d] - u_imag * ahead[3 + d]
-                more_imag = u_real * ahead[3 + d] + u_imag * ahead[d]
-                real = more_real if real is None else real + more_real
-                imag = more_imag if imag is None else imag + more_imag
-            real_rows.append(real.astype(BF16))
-            imag_rows.append(imag.astype(BF16))
-        columns.append(jnp.concatenate(real_rows + imag_rows, axis=0))
-        columns.append(jnp.concatenate(imag_rows + [-r for r in real_rows], axis=0))
+        columns.append(jnp.concatenate(derived, axis=0))
+        columns.append(jnp.concatenate(derived[3:] + [-d for d in derived[:3]], axis=0))
     norm_scale = 1.0 / math.sqrt(24.0 * sites)
     product = dot(
-        jnp.concatenate(fields, axis=0), jnp.concatenate(columns, axis=1), (((0,), (0,)), ((), ()))
+        jnp.concatenate([h.astype(BF16) for h in here], axis=0),
+        jnp.concatenate(columns, axis=1),
+        (((0,), (0,)), ((), ())),
     ) * norm_scale
     for mu in range(3):
-        a_real = product[:, (2 * mu) * modes : (2 * mu + 1) * modes]
-        a_imag = product[:, (2 * mu + 1) * modes : (2 * mu + 2) * modes]
-        e_all[mu, 0] = a_real - a_real.T
-        e_all[mu, 1] = a_imag + a_imag.T
+        for ri in range(2):
+            at = (2 * mu + ri) * modes
+            e_all[mu, ri] = product[:, at : at + modes]
 
     def picked(gamma, part):
         return e_all[dirs_ref[gamma], part].astype(BF16).astype(F32)
@@ -238,15 +273,14 @@
         return copy
 
     z_copies = []
-    real_sum, imag_sum = 0.0, 0.0
+    lines = 0.0
     for i in range(CHUNKS):
         wide = first_rows(p_ref[i * part : (i + 1) * part, :], m_ref[...])
         span = pl.ds(pl.multiple_of(first_row + i * part, part), part)
         f_all[span, :] = wide.astype(BF16)
         z_copies.append(to_below(f_all.at[span], f_next.at[pl.ds(i * part, part)], i))
-        more_real, more_imag = diagonal_sums(wide, first_row + i * part)
-        real_sum, imag_sum = real_sum + more_real, imag_sum + more_imag
-    diagonals += [real_sum, imag_sum]
+        lines += diagonal_lines(wide, first_row + i * part)
+    diagonals.append(lines)
 
     for j in range(1, S):
         other = lax.rem(s + j, S)
@@ -277,36 +311,38 @@
                 mine_columns = jnp.where(k == i, block[:, i * half : (i + 1) * half], mine_columns)
             elem_ref[:, mu, ri, :] = mine_columns
 
-    real_sum, imag_sum = 0.0, 0.0
+    lane = lax.broadcasted_iota(jnp.int32, (2, 128), 1)
+    wanted = jnp.full((2, 128), -1, jnp.int32)
+    for n in range(src_ref.shape[0]):
+        wanted = jnp.where(lane == n, src_ref[n], wanted)
+    tile_row = lax.broadcasted_iota(jnp.int32, (8, 128), 0)
+    weight = jnp.zeros((8, 128), F32)
+    for o in range(3):
+        count = sum(jnp.where(off_ref[j] == o, 1, 0) for j in range(off_ref.shape[0]))
+        weight = jnp.where(lax.div(tile_row, 2) == o, count.astype(F32), weight)
+
+    lines = 0.0
     for i in range(CHUNKS):
         span = pl.ds(i * part, part)
         z_copies[i].wait_recv()
         wide = complex_rows(f_next[span, :], f_all[...])
         s_own[span, :] = wide.astype(BF16)
         z_copies.append(to_below(s_own.at[span], s_next.at[span], CHUNKS + i))
-        more_real, more_imag = diagonal_sums(wide, first_row + i * part)
-        real_sum, imag_sum = real_sum + more_real, imag_sum + more_imag
-    diagonals += [real_sum, imag_sum]
-
-    real_sum, imag_sum = 0.0, 0.0
+        lines += diagonal_lines(wide, first_row + i * part)
+    diagonals.append(lines)
+
+    lines = 0.0
     for i in range(CHUNKS):
         span = pl.ds(i * part, part)
         z_copies[CHUNKS + i].wait_recv()
         wide = complex_rows(s_next[span, :], f_all[...])
         chain_ref[span, :] = (wide * math.sqrt(order)).astype(BF16)
-        more_real, more_imag = diagonal_sums(wide, first_row + i * part)
-        real_sum, imag_sum = real_sum + more_real, imag_sum + more_imag
-    diagonals += [real_sum, imag_sum]
-
-    tile_row = lax.broadcasted_iota(jnp.int32, (8, 128), 0)
-    tile_lane = lax.broadcasted_iota(jnp.int32, (8, 128), 1)
-    tile = jnp.zeros((8, 128), F32)
-    for o in range(3):
-        for ri in range(2):
-            tile = jnp.where((tile_row == o) & (tile_lane == ri), diagonals[2 * o + ri], tile)
+        lines += diagonal_lines(wide, first_row + i * part)
+    diagonals.append(lines)
+
+    t_all[t * G + rank] = jnp.concatenate(diagonals + [jnp.zeros((2, 128), F32)], axis=0)
     total = T * G
     me = t * G + rank
-    t_all[me] = tile
 
     def trace_copy(j):
         other = lax.rem(me + j, total)
@@ -333,35 +369,26 @@
 
     lax.fori_loop(1, total, wait_trace, 0)
 
-    counts = []
-    for o in range(3):
-        count = 0
-        for j in range(off_ref.shape[0]):
-            count = count + jnp.where(off_ref[j] == o, 1, 0)
-        counts.append(count.astype(F32))
-    weight = jnp.zeros((8, 128), F32)
-    for o in range(3):
-        weight = jnp.where(tile_row == o, counts[o], weight)
-    sources = src_ref.shape[0]
-    out_row = lax.broadcasted_iota(jnp.int32, (sources, 128), 0)
-    wanted = jnp.zeros((sources, 128), jnp.int32)
-    for n in range(sources):
-        wanted = jnp.where(out_row == n, src_ref[n], wanted)
-
     def add_time(i, acc):
         summed = t_all[i * G]
         for g in range(1, G):
             summed = summed + t_all[i * G + g]
-        line = jnp.sum(summed * weight, axis=0, keepdims=True)
-        return acc + jnp.where(wanted == i, line, 0.0)
-
-    found = lax.fori_loop(0, T, add_time, jnp.zeros((sources, 128), F32))
+        weighted = jnp.sum(summed * weight, axis=1, keepdims=True)
+        pair = weighted[0:2] + weighted[2:4] + weighted[4:6]
+        return acc + jnp.where(wanted == i, pair, 0.0)
+
+    found = lax.fori_loop(0, T, add_time, jnp.zeros((2, 128), F32))
     corr_ref[...] = found[:, : corr_ref.shape[1]]
 
     for copy in sends:
         copy.wait_send()
     for copy in z_copies:
         copy.wait_send()
+
+
+def copy_kernel(*refs):
+    for source, target in zip(refs[:3], refs[3:]):
+        target[...] = source[...]
 
 
 def on_device(
@@ -371,11 +398,11 @@
     _, _, _, planes, side, _, modes = eigenvectors.shape
     slab = planes * side * side
     vectors = eigenvectors.reshape((6, slab, modes))
-    links = gauge_links.reshape((54, slab))
+    links = jnp.swapaxes(gauge_links, 5, 6).reshape((54 * side * side, planes))
     peram = perambulators[0]
     rows, width = peram.shape
     order = width // 2
-    table = jnp.asarray(shift_table(planes * S, side), BF16)
+    table = jnp.asarray(shift_table(S, planes, side), BF16)
     vmem = pl.BlockSpec(memory_space=pltpu.VMEM)
     smem = pl.BlockSpec(memory_space=pltpu.SMEM)
     dma = pltpu.SemaphoreType.DMA
@@ -384,13 +411,14 @@
         out_shape=(
             jax.ShapeDtypeStruct((modes // S, 3, 2, modes // K), F32),
             jax.ShapeDtypeStruct((rows, width), BF16),
-            jax.ShapeDtypeStruct((source_times.shape[0], 2), F32),
+            jax.ShapeDtypeStruct((2, source_times.shape[0]), F32),
         ),
         in_specs=[vmem, vmem, vmem, vmem, smem, smem, smem],
         out_specs=(vmem, vmem, vmem),
         scratch_shapes=[
             pltpu.VMEM((S, 6, slab, modes), BF16),
-            pltpu.VMEM((S, 54, slab), BF16),
+            pltpu.VMEM((planes, 54 * side * side), BF16),
+            pltpu.VMEM((S, planes, 54 * side * side), BF16),
             pltpu.VMEM((order, width), BF16),
             pltpu.VMEM((3, 2, modes, modes), F32),
             pltpu.VMEM((2 * modes, 4 * modes), BF16),
@@ -414,7 +442,13 @@
         ],
         compiler_params=pltpu.CompilerParams(collective_id=0, has_side_effects=True),
     )(vectors, links, peram, table, source_times, insert_offsets, derivative_dirs)
-    return (elementals[None], chain[None], correlator)
+    elementals, chain, correlator = pl.pallas_call(
+        copy_kernel,
+        out_shape=tuple(jax.ShapeDtypeStruct(a.shape, a.dtype) for a in (elementals, chain, correlator)),
+        in_specs=[vmem] * 3,
+        out_specs=(vmem,) * 3,
+    )(elementals, chain, correlator)
+    return (elementals[None], chain[None], correlator.T)
 
 
 def solution(mesh):

time: 38.3 us -> 34.8 us (0.909)
  local copies, waits for them, and re-layouts: 5.67 us -> 0 us
  Pallas kernels: 31.7 us -> 34 us
    unnamed x6 -> x0, local copies, waits for them, and re-layouts: 4.95 us -> none
    pallas_call x0 -> x1, Pallas kernels: none -> 1.86 us  [on_device(): pl.pallas_call(copy_kernel, out_shape=tuple((jax.ShapeDtypeStruct(a.shape...]
    reshape x1 -> x0, local copies, waits for them, and re-layouts: 0.72 us -> none  [on_device(): links = gauge_links.reshape((54, slab))]
    pallas_call x1, Pallas kernels: 31.7 us -> 32.2 us  [on_device(): pl.pallas_call(functools.partial(kernel, sizes), out_shape=(jax.ShapeDtyp...]
where the time goes in v2:
time: 34.8 us; the launch traced here: 34.7 us
  Pallas kernels  34 us (98%)
  between operations  0.64 us (2%)
    pallas_call x1, Pallas kernels, on_device(): pl.pallas_call(functools.partial(kernel, sizes), out_shape=(jax.ShapeDtyp...  32.2 us
    pallas_call x1, Pallas kernels, on_device(): pl.pallas_call(copy_kernel, out_shape=tuple((jax.ShapeDtypeStruct(a.shape...  1.86 us

profile of v2, /device:TPU:0, one launch (start us, length us, event | category | flops | bytes accessed | tf_op | source)
XLA Modules:
  0.0 34.7 jit_solution(3970974942170698811)
XLA Ops:
  0.6 32.2 %shard_map.94 = (f32[64,3,2,64]{3,2,1,0:T(2,128)}, bf16[128,1024]{1,0:T(8,128)(2,1)}, f32[2,16]{1,0:T(2,128)}) custom-call(bf16[6,32,128]{2,1,0:T(8,128)(2,1)} %bitcast.10, bf16[216,8]{1,0:T(8,128)(2,1)} %bitcast.9, bf16[128,1024]{1,0:T(8,128)(2,1)} %bitcast.8, bf16[448,64]{1,0:T(8,128)(2,1)} %constant.2.clone.table_ref, s32[16]{0:T(128)} %src_ref.1, ...), custom_call_target="tpu_custom_call" | custom-call | tf_op jit(solution)/shard_map/pallas_call | solution.py:409
  32.8 1.9 %shard_map.95 = (f32[64,3,2,64]{3,2,1,0:T(2,128)}, bf16[128,1024]{1,0:T(8,128)(2,1)}, f32[2,16]{1,0:T(2,128)}) custom-call(f32[64,3,2,64]{3,2,1,0:T(2,128)} %get-tuple-element.9.refs_0_, bf16[128,1024]{1,0:T(8,128)(2,1)} %get-tuple-element.10.refs_1_, f32[2,16]{1,0:T(2,128)} %get-tuple-element.11.refs_2_), custom_call_target="tpu_custom_call" | custom-call | tf_op jit(solution)/shard_map/pallas_call | solution.py:445

commit v3 on v2

--- a/solution.py
+++ b/solution.py
@@ -13,6 +13,7 @@
 F32 = jnp.float32
 BF16 = jnp.bfloat16
 CHUNKS = 4
+PIECES = 2
 
 
 def dot(a, b, dims=(((1,), (0,)), ((), ()))):
@@ -103,6 +104,9 @@
     elem_ref,
     chain_ref,
     corr_ref,
+    l_in,
+    table_in,
+    in_sem,
     v_all,
     l_own,
     l_all,
@@ -138,13 +142,20 @@
     mine = pl.ds(pl.multiple_of(first_row, rows), rows)
     below, above = lax.rem(t + T - 1, T), lax.rem(t + 1, T)
 
+    loads = [
+        pltpu.make_async_copy(source, target, in_sem.at[i])
+        for i, (source, target) in enumerate(
+            (
+                (l_ref, l_in),
+                (v_ref, v_all.at[s]),
+                (p_ref, p_all.at[mine]),
+                (table_ref, table_in),
+            )
+        )
+    ]
+    for load in loads:
+        load.start()
     planes = l_ref.shape[1]
-    eye = (
-        lax.broadcasted_iota(jnp.int32, (planes, planes), 0)
-        == lax.broadcasted_iota(jnp.int32, (planes, planes), 1)
-    ).astype(F32).astype(BF16)
-    l_own[...] = dot(eye, l_ref[...], (((1,), (1,)), ((), ()))).astype(BF16)
-
     barrier = pltpu.get_barrier_semaphore()
     for j in range(1, G):
         other = lax.rem(rank + j, G)
@@ -156,13 +167,21 @@
         )
     for target in (below, above):
         pl.semaphore_signal(barrier, inc=1, device_id={"tm": target}, device_id_type=MESH)
+    eye = (
+        lax.broadcasted_iota(jnp.int32, (planes, planes), 0)
+        == lax.broadcasted_iota(jnp.int32, (planes, planes), 1)
+    ).astype(F32).astype(BF16)
+    loads[0].wait()
+    l_own[...] = dot(eye, l_in[...], (((1,), (1,)), ((), ()))).astype(BF16)
+    for load in loads[1:]:
+        load.wait()
     pl.semaphore_wait(barrier, G + 1)
 
     sends = []
     for j in range(1, S):
         other = lax.rem(s + j, S)
         for source, target, send_sem, recv_sem in (
-            (v_ref, v_all.at[s], v_send, v_recv),
+            (v_all.at[s], v_all.at[s], v_send, v_recv),
             (l_own, l_all.at[s], l_send, l_recv),
         ):
             copy = pltpu.make_async_remote_copy(
@@ -171,22 +190,29 @@
             )
             copy.start()
             sends.append(copy)
-    for j in range(1, S):
-        other = lax.rem(s + j, S)
-        copy = pltpu.make_async_remote_copy(
-            p_ref, p_all.at[mine], p_send.at[j], p_recv.at[s],
-            device_id={"space": other}, device_id_type=MESH,
-        )
-        copy.start()
-        sends.append(copy)
-    for i in range(1, K):
-        copy = pltpu.make_async_remote_copy(
-            p_ref, p_all.at[mine], q_send.at[0, i], q_recv.at[rank],
-            device_id={"spin": lax.rem(k + i, K)}, device_id_type=MESH,
-        )
-        copy.start()
-        sends.append(copy)
-    v_all[s] = v_ref[...]
+    piece = rows // PIECES
+
+    def block_of(owner, c):
+        return pl.ds(pl.multiple_of(owner * rows + c * piece, piece), piece)
+
+    for c in range(PIECES):
+        block = p_all.at[block_of(rank, c)]
+        for j in range(1, S):
+            copy = pltpu.make_async_remote_copy(
+                block, block, p_send.at[j, c], p_recv.at[s, c],
+                device_id={"space": lax.rem(s + j, S)}, device_id_type=MESH,
+            )
+            copy.start()
+            sends.append(copy)
+    for c in range(PIECES):
+        block = p_all.at[block_of(rank, c)]
+        for i in range(1, K):
+            copy = pltpu.make_async_remote_copy(
+                block, block, q_send.at[0, i, c], q_recv.at[rank, c],
+                device_id={"spin": lax.rem(k + i, K)}, device_id_type=MESH,
+            )
+            copy.start()
+            sends.append(copy)
     l_all[s] = l_own[...]
 
     for j in range(1, S):
@@ -198,7 +224,7 @@
     sites = S * slab
     cells = slab // planes
     fields = [jnp.concatenate([v_all[i, j] for i in range(S)], axis=0) for j in range(6)]
-    moved = dot(table_ref[: 4 * sites, :], jnp.concatenate(fields, axis=1))
+    moved = dot(table_in[: 4 * sites, :], jnp.concatenate(fields, axis=1))
 
     def field(block, j):
         return moved[block * sites : (block + 1) * sites, j * modes : (j + 1) * modes]
@@ -230,7 +256,7 @@
                 adjoint[column] += real * here[row] + imag * here[3 + row]
                 adjoint[3 + column] += real * here[3 + row] - imag * here[row]
         behind = dot(
-            table_ref[(4 + mu) * sites : (5 + mu) * sites, :],
+            table_in[(4 + mu) * sites : (5 + mu) * sites, :],
             jnp.concatenate([a.astype(BF16) for a in adjoint], axis=1),
         )
         derived = [
@@ -275,31 +301,65 @@
     z_copies = []
     lines = 0.0
     for i in range(CHUNKS):
-        wide = first_rows(p_ref[i * part : (i + 1) * part, :], m_ref[...])
         span = pl.ds(pl.multiple_of(first_row + i * part, part), part)
+        wide = first_rows(p_all[span, :], m_ref[...])
         f_all[span, :] = wide.astype(BF16)
         z_copies.append(to_below(f_all.at[span], f_next.at[pl.ds(i * part, part)], i))
         lines += diagonal_lines(wide, first_row + i * part)
     diagonals.append(lines)
 
-    for j in range(1, S):
-        other = lax.rem(s + j, S)
-        block = pl.ds(pl.multiple_of((other * K + k) * rows, rows), rows)
-        pltpu.make_async_copy(p_all.at[block], p_all.at[block], p_recv.at[other]).wait()
-        for i in range(1, K):
-            copy = pltpu.make_async_remote_copy(
-                p_all.at[block], p_all.at[block], q_send.at[j, i], q_recv.at[other * K + k],
-                device_id={"spin": lax.rem(k + i, K)}, device_id_type=MESH,
-            )
-            copy.start()
-            sends.append(copy)
+    def arrived(owner, c, sem):
+        block = p_all.at[block_of(owner, c)]
+        pltpu.make_async_copy(block, block, sem).wait()
+
+    def multiply(owner, c):
+        block = block_of(owner, c)
         f_all[block, :] = first_rows(p_all[block, :], m_ref[...]).astype(BF16)
-    for j in range(S):
-        for i in range(1, K):
-            owner = lax.rem(s + j, S) * K + lax.rem(k + i, K)
-            block = pl.ds(pl.multiple_of(owner * rows, rows), rows)
-            pltpu.make_async_copy(p_all.at[block], p_all.at[block], q_recv.at[owner]).wait()
-            f_all[block, :] = first_rows(p_all[block, :], m_ref[...]).astype(BF16)
+
+    for i in range(1, K):
+        owner = s * K + lax.rem(k + i, K)
+        for c in range(PIECES):
+            arrived(owner, c, q_recv.at[owner, c])
+            multiply(owner, c)
+    for c in range(PIECES):
+        for j in range(1, S):
+            other = lax.rem(s + j, S)
+            owner = other * K + k
+            arrived(owner, c, p_recv.at[other, c])
+            for i in range(1, K):
+                block = p_all.at[block_of(owner, c)]
+                copy = pltpu.make_async_remote_copy(
+                    block, block, q_send.at[j, i, c], q_recv.at[owner, c],
+                    device_id={"spin": lax.rem(k + i, K)}, device_id_type=MESH,
+                )
+                copy.start()
+                sends.append(copy)
+            multiply(owner, c)
+        for j in range(1, S):
+            for i in range(1, K):
+                owner = lax.rem(s + j, S) * K + lax.rem(k + i, K)
+                arrived(owner, c, q_recv.at[owner, c])
+                multiply(owner, c)
+
+    lane = lax.broadcasted_iota(jnp.int32, (2, 128), 1)
+    wanted = jnp.full((2, 128), -1, jnp.int32)
+    for n in range(src_ref.shape[0]):
+        wanted = jnp.where(lane == n, src_ref[n], wanted)
+    tile_row = lax.broadcasted_iota(jnp.int32, (8, 128), 0)
+    weight = jnp.zeros((8, 128), F32)
+    for o in range(3):
+        count = sum(jnp.where(off_ref[j] == o, 1, 0) for j in range(off_ref.shape[0]))
+        weight = jnp.where(lax.div(tile_row, 2) == o, count.astype(F32), weight)
+
+    lines = 0.0
+    for i in range(CHUNKS):
+        span = pl.ds(i * part, part)
+        z_copies[i].wait_recv()
+        wide = complex_rows(f_next[span, :], f_all[...])
+        s_own[span, :] = wide.astype(BF16)
+        z_copies.append(to_below(s_own.at[span], s_next.at[span], CHUNKS + i))
+        lines += diagonal_lines(wide, first_row + i * part)
+    diagonals.append(lines)
 
     share, half = elem_ref.shape[0], elem_ref.shape[3]
     own_rows = pl.ds(pl.multiple_of(s * share, share), share)
@@ -310,26 +370,6 @@
             for i in range(1, K):
                 mine_columns = jnp.where(k == i, block[:, i * half : (i + 1) * half], mine_columns)
             elem_ref[:, mu, ri, :] = mine_columns
-
-    lane = lax.broadcasted_iota(jnp.int32, (2, 128), 1)
-    wanted = jnp.full((2, 128), -1, jnp.int32)
-    for n in range(src_ref.shape[0]):
-        wanted = jnp.where(lane == n, src_ref[n], wanted)
-    tile_row = lax.broadcasted_iota(jnp.int32, (8, 128), 0)
-    weight = jnp.zeros((8, 128), F32)
-    for o in range(3):
-        count = sum(jnp.where(off_ref[j] == o, 1, 0) for j in range(off_ref.shape[0]))
-        weight = jnp.where(lax.div(tile_row, 2) == o, count.astype(F32), weight)
-
-    lines = 0.0
-    for i in range(CHUNKS):
-        span = pl.ds(i * part, part)
-        z_copies[i].wait_recv()
-        wide = complex_rows(f_next[span, :], f_all[...])
-        s_own[span, :] = wide.astype(BF16)
-        z_copies.append(to_below(s_own.at[span], s_next.at[span], CHUNKS + i))
-        lines += diagonal_lines(wide, first_row + i * part)
-    diagonals.append(lines)
 
     lines = 0.0
     for i in range(CHUNKS):
@@ -387,8 +427,13 @@
 
 
 def copy_kernel(*refs):
-    for source, target in zip(refs[:3], refs[3:]):
-        target[...] = source[...]
+    copies = [
+        pltpu.make_async_copy(refs[i], refs[3 + i], refs[6].at[i]) for i in range(3)
+    ]
+    for copy in copies:
+        copy.start()
+    for copy in copies:
+        copy.wait()
 
 
 def on_device(
@@ -404,18 +449,22 @@
     order = width // 2
     table = jnp.asarray(shift_table(S, planes, side), BF16)
     vmem = pl.BlockSpec(memory_space=pltpu.VMEM)
+    hbm = pl.BlockSpec(memory_space=pltpu.HBM)
     smem = pl.BlockSpec(memory_space=pltpu.SMEM)
     dma = pltpu.SemaphoreType.DMA
     elementals, chain, correlator = pl.pallas_call(
         functools.partial(kernel, sizes),
         out_shape=(
-            jax.ShapeDtypeStruct((modes // S, 3, 2, modes // K), F32),
-            jax.ShapeDtypeStruct((rows, width), BF16),
-            jax.ShapeDtypeStruct((2, source_times.shape[0]), F32),
+            pltpu.VMEM((modes // S, 3, 2, modes // K), F32),
+            pltpu.VMEM((rows, width), BF16),
+            pltpu.VMEM((2, source_times.shape[0]), F32),
         ),
-        in_specs=[vmem, vmem, vmem, vmem, smem, smem, smem],
+        in_specs=[hbm, hbm, hbm, hbm, smem, smem, smem],
         out_specs=(vmem, vmem, vmem),
         scratch_shapes=[
+            pltpu.VMEM(links.shape, BF16),
+            pltpu.VMEM(table.shape, BF16),
+            dma((4,)),
             pltpu.VMEM((S, 6, slab, modes), BF16),
             pltpu.VMEM((planes, 54 * side * side), BF16),
             pltpu.VMEM((S, planes, 54 * side * side), BF16),
@@ -431,10 +480,10 @@
             dma((S,)),
             dma((S,)),
             dma((S,)),
-            dma((S,)),
-            dma((S,)),
-            dma((S, K)),
-            dma((S * K,)),
+            dma((S, PIECES)),
+            dma((S, PIECES)),
+            dma((S, K, PIECES)),
+            dma((S * K, PIECES)),
             dma((2 * CHUNKS,)),
             dma((2 * CHUNKS,)),
             dma((T * S * K,)),
@@ -446,8 +495,9 @@
         copy_kernel,
         out_shape=tuple(jax.ShapeDtypeStruct(a.shape, a.dtype) for a in (elementals, chain, correlator)),
         in_specs=[vmem] * 3,
-        out_specs=(vmem,) * 3,
-    )(elementals, chain, correlator)
+        out_specs=(pl.BlockSpec(memory_space=pl.ANY),) * 3,
+        scratch_shapes=[dma((3,))],
+    )(*(pltpu.with_memory_space_constraint(a, pltpu.VMEM) for a in (elementals, chain, correlator)))
     return (elementals[None], chain[None], correlator.T)
 
 

time: 34.8 us -> 31.8 us (0.914)
  Pallas kernels: 34 us -> 31 us
    pallas_call x1, Pallas kernels: 32.2 us -> 30.2 us  [on_device(): pl.pallas_call(functools.partial(kernel, sizes), out_shape=(pltpu.VMEM((m...]
    pallas_call x1, Pallas kernels: 1.86 us -> 0.8 us  [on_device(): pl.pallas_call(copy_kernel, out_shape=tuple((jax.ShapeDtypeStruct(a.shape...]
where the time goes in v3:
time: 31.8 us; the launch traced here: 31.6 us
  Pallas kernels  31 us (97%)
  between operations  0.64 us (2%)
    pallas_call x1, Pallas kernels, on_device(): pl.pallas_call(functools.partial(kernel, sizes), out_shape=(pltpu.VMEM((m...  30.2 us
    pallas_call x1, Pallas kernels, on_device(): pl.pallas_call(copy_kernel, out_shape=tuple((jax.ShapeDtypeStruct(a.shape...  0.8 us

profile of v3, /device:TPU:0, one launch (start us, length us, event | category | flops | bytes accessed | tf_op | source)
XLA Modules:
  0.0 31.6 jit_solution(6672523263121583406)
XLA Ops:
  0.6 30.2 %shard_map.94 = (f32[64,3,2,64]{3,2,1,0:T(2,128)S(1)}, bf16[128,1024]{1,0:T(8,128)(2,1)S(1)}, f32[2,16]{1,0:T(2,128)S(1)}) custom-call(bf16[6,32,128]{2,1,0:T(8,128)(2,1)} %bitcast.10, bf16[216,8]{1,0:T(8,128)(2,1)} %bitcast.9, bf16[128,1024]{1,0:T(8,128)(2,1)} %bitcast.8, bf16[448,64]{1,0:T(8,128)(2,1)} %constant.2.clone.table_ref, s32[16]{0:T(128)} %src_ref.1, ...), custom_call_target="tpu_custom_call" | custom-call | tf_op jit(solution)/shard_map/pallas_call | solution.py:455
  30.8 0.8 %shard_map.95 = (f32[64,3,2,64]{3,2,1,0:T(2,128)}, bf16[128,1024]{1,0:T(8,128)(2,1)}, f32[2,16]{1,0:T(2,128)}) custom-call(f32[64,3,2,64]{3,2,1,0:T(2,128)S(1)} %get-tuple-element.9.refs_0_, bf16[128,1024]{1,0:T(8,128)(2,1)S(1)} %get-tuple-element.10.refs_1_, f32[2,16]{1,0:T(2,128)S(1)} %get-tuple-element.11.refs_2_), custom_call_target="tpu_custom_call" | custom-call | tf_op jit(solution)/shard_map/pallas_call | solution.py:494

commit v4 on v3

--- a/solution.py
+++ b/solution.py
@@ -12,7 +12,7 @@
 MESH = pl.DeviceIdType.MESH
 F32 = jnp.float32
 BF16 = jnp.bfloat16
-CHUNKS = 4
+CHUNK_ROWS = 16
 PIECES = 2
 
 
@@ -126,6 +126,7 @@
     p_recv,
     q_send,
     q_recv,
+    ready,
     z_send,
     z_recv,
     t_send,
@@ -165,8 +166,24 @@
             device_id={"tm": t, "space": lax.div(other, K), "spin": lax.rem(other, K)},
             device_id_type=MESH,
         )
-    for target in (below, above):
-        pl.semaphore_signal(barrier, inc=1, device_id={"tm": target}, device_id_type=MESH)
+    pl.semaphore_signal(barrier, inc=1, device_id={"tm": below}, device_id_type=MESH)
+    entered = G
+    if T > 4:
+        def announce(j, carry):
+            other = lax.rem(t * G + rank + j, T * G)
+            group = lax.rem(other, G)
+            pl.semaphore_signal(
+                barrier,
+                inc=1,
+                device_id={
+                    "tm": lax.div(other, G), "space": lax.div(group, K), "spin": lax.rem(group, K)
+                },
+                device_id_type=MESH,
+            )
+            return carry
+
+        lax.fori_loop(1, T * G, announce, 0)
+        entered += T * G - 1
     eye = (
         lax.broadcasted_iota(jnp.int32, (planes, planes), 0)
         == lax.broadcasted_iota(jnp.int32, (planes, planes), 1)
@@ -175,7 +192,8 @@
     l_own[...] = dot(eye, l_in[...], (((1,), (1,)), ((), ()))).astype(BF16)
     for load in loads[1:]:
         load.wait()
-    pl.semaphore_wait(barrier, G + 1)
+    pl.semaphore_wait(barrier, entered)
+    pl.semaphore_signal(ready, inc=1, device_id={"tm": above}, device_id_type=MESH)
 
     sends = []
     for j in range(1, S):
@@ -287,7 +305,8 @@
         axis=0,
     ).astype(BF16)
 
-    part = rows // CHUNKS
+    chunks = max(1, rows // CHUNK_ROWS)
+    part = rows // chunks
     diagonals = []
 
     def to_below(source, target, index):
@@ -300,10 +319,12 @@
 
     z_copies = []
     lines = 0.0
-    for i in range(CHUNKS):
+    for i in range(chunks):
         span = pl.ds(pl.multiple_of(first_row + i * part, part), part)
         wide = first_rows(p_all[span, :], m_ref[...])
         f_all[span, :] = wide.astype(BF16)
+        if i == 0:
+            pl.semaphore_wait(ready, 1)
         z_copies.append(to_below(f_all.at[span], f_next.at[pl.ds(i * part, part)], i))
         lines += diagonal_lines(wide, first_row + i * part)
     diagonals.append(lines)
@@ -352,12 +373,12 @@
         weight = jnp.where(lax.div(tile_row, 2) == o, count.astype(F32), weight)
 
     lines = 0.0
-    for i in range(CHUNKS):
+    for i in range(chunks):
         span = pl.ds(i * part, part)
         z_copies[i].wait_recv()
         wide = complex_rows(f_next[span, :], f_all[...])
         s_own[span, :] = wide.astype(BF16)
-        z_copies.append(to_below(s_own.at[span], s_next.at[span], CHUNKS + i))
+        z_copies.append(to_below(s_own.at[span], s_next.at[span], chunks + i))
         lines += diagonal_lines(wide, first_row + i * part)
     diagonals.append(lines)
 
@@ -372,9 +393,9 @@
             elem_ref[:, mu, ri, :] = mine_columns
 
     lines = 0.0
-    for i in range(CHUNKS):
+    for i in range(chunks):
         span = pl.ds(i * part, part)
-        z_copies[CHUNKS + i].wait_recv()
+        z_copies[chunks + i].wait_recv()
         wide = complex_rows(s_next[span, :], f_all[...])
         chain_ref[span, :] = (wide * math.sqrt(order)).astype(BF16)
         lines += diagonal_lines(wide, first_row + i * part)
@@ -447,6 +468,7 @@
     peram = perambulators[0]
     rows, width = peram.shape
     order = width // 2
+    chunks = max(1, rows // CHUNK_ROWS)
     table = jnp.asarray(shift_table(S, planes, side), BF16)
     vmem = pl.BlockSpec(memory_space=pltpu.VMEM)
     hbm = pl.BlockSpec(memory_space=pltpu.HBM)
@@ -484,8 +506,9 @@
             dma((S, PIECES)),
             dma((S, K, PIECES)),
             dma((S * K, PIECES)),
-            dma((2 * CHUNKS,)),
-            dma((2 * CHUNKS,)),
+            pltpu.SemaphoreType.REGULAR,
+            dma((2 * chunks,)),
+            dma((2 * chunks,)),
             dma((T * S * K,)),
             dma((T * S * K,)),
         ],

time: 31.8 us -> 30.6 us (0.962)
  Pallas kernels: 31 us -> 29.8 us
    pallas_call x1, Pallas kernels: 30.2 us -> 29 us  [on_device(): pl.pallas_call(functools.partial(kernel, sizes), out_shape=(pltpu.VMEM((m...]
where the time goes in v4:
time: 30.6 us; the launch traced here: 30.5 us
  Pallas kernels  29.8 us (97%)
  between operations  0.64 us (2%)
    pallas_call x1, Pallas kernels, on_device(): pl.pallas_call(functools.partial(kernel, sizes), out_shape=(pltpu.VMEM((m...  29 us
    pallas_call x1, Pallas kernels, on_device(): pl.pallas_call(copy_kernel, out_shape=tuple((jax.ShapeDtypeStruct(a.shape...  0.8 us

profile of v4, /device:TPU:0, one launch (start us, length us, event | category | flops | bytes accessed | tf_op | source)
XLA Modules:
  0.0 30.5 jit_solution(14216716105320120870)
XLA Ops:
  0.6 29.0 %shard_map.94 = (f32[64,3,2,64]{3,2,1,0:T(2,128)S(1)}, bf16[128,1024]{1,0:T(8,128)(2,1)S(1)}, f32[2,16]{1,0:T(2,128)S(1)}) custom-call(bf16[6,32,128]{2,1,0:T(8,128)(2,1)} %bitcast.10, bf16[216,8]{1,0:T(8,128)(2,1)} %bitcast.9, bf16[128,1024]{1,0:T(8,128)(2,1)} %bitcast.8, bf16[448,64]{1,0:T(8,128)(2,1)} %constant.2.clone.table_ref, s32[16]{0:T(128)} %src_ref.1, ...), custom_call_target="tpu_custom_call" | custom-call | tf_op jit(solution)/shard_map/pallas_call | solution.py:477
  29.7 0.8 %shard_map.95 = (f32[64,3,2,64]{3,2,1,0:T(2,128)}, bf16[128,1024]{1,0:T(8,128)(2,1)}, f32[2,16]{1,0:T(2,128)}) custom-call(f32[64,3,2,64]{3,2,1,0:T(2,128)S(1)} %get-tuple-element.9.refs_0_, bf16[128,1024]{1,0:T(8,128)(2,1)S(1)} %get-tuple-element.10.refs_1_, f32[2,16]{1,0:T(2,128)S(1)} %get-tuple-element.11.refs_2_), custom_call_target="tpu_custom_call" | custom-call | tf_op jit(solution)/shard_map/pallas_call | solution.py:517

commit v5 on v4

--- a/solution.py
+++ b/solution.py
@@ -13,7 +13,7 @@
 F32 = jnp.float32
 BF16 = jnp.bfloat16
 CHUNK_ROWS = 16
-PIECES = 2
+PIECES = 4
 
 
 def dot(a, b, dims=(((1,), (0,)), ((), ()))):
@@ -416,19 +416,39 @@
             device_id_type=MESH,
         )
 
-    def start_trace(j, carry):
-        trace_copy(j)[1].start()
-        return carry
-
-    lax.fori_loop(1, total, start_trace, 0)
-
-    def wait_trace(j, carry):
-        other, copy = trace_copy(j)
-        copy.wait_send()
-        pltpu.make_async_copy(t_all.at[other], t_all.at[other], t_recv.at[other]).wait()
-        return carry
-
-    lax.fori_loop(1, total, wait_trace, 0)
+    if total <= 16:
+
+        def wrapped(value, size):
+            return jnp.where(value >= size, value - size, value)
+
+        started = []
+        for j in range(1, total):
+            at = (
+                wrapped(t + j // G, T), wrapped(s + (j % G) // K, S), wrapped(k + j % K, K)
+            )
+            copy = pltpu.make_async_remote_copy(
+                t_all.at[me], t_all.at[me], t_send.at[j], t_recv.at[me],
+                device_id=dict(zip(("tm", "space", "spin"), at)), device_id_type=MESH,
+            )
+            copy.start()
+            started.append((copy, (at[0] * S + at[1]) * K + at[2]))
+        for copy, other in started:
+            copy.wait_send()
+            pltpu.make_async_copy(t_all.at[other], t_all.at[other], t_recv.at[other]).wait()
+    else:
+        def start_trace(j, carry):
+            trace_copy(j)[1].start()
+            return carry
+
+        lax.fori_loop(1, total, start_trace, 0)
+
+        def wait_trace(j, carry):
+            other, copy = trace_copy(j)
+            copy.wait_send()
+            pltpu.make_async_copy(t_all.at[other], t_all.at[other], t_recv.at[other]).wait()
+            return carry
+
+        lax.fori_loop(1, total, wait_trace, 0)
 
     def add_time(i, acc):
         summed = t_all[i * G]

time: 30.6 us -> 32.1 us (1.049)
  Pallas kernels: 29.8 us -> 31.3 us
    pallas_call x1, Pallas kernels: 29 us -> 30.5 us  [on_device(): pl.pallas_call(functools.partial(kernel, sizes), out_shape=(pltpu.VMEM((m...]
where the time goes in v5:
time: 32.1 us; the launch traced here: 32 us
  Pallas kernels  31.3 us (98%)
  between operations  0.64 us (2%)
    pallas_call x1, Pallas kernels, on_device(): pl.pallas_call(functools.partial(kernel, sizes), out_shape=(pltpu.VMEM((m...  30.5 us
    pallas_call x1, Pallas kernels, on_device(): pl.pallas_call(copy_kernel, out_shape=tuple((jax.ShapeDtypeStruct(a.shape...  0.8 us

profile of v5, /device:TPU:0, one launch (start us, length us, event | category | flops | bytes accessed | tf_op | source)
XLA Modules:
  0.0 32.0 jit_solution(16162501540204113197)
XLA Ops:
  0.6 30.5 %shard_map.94 = (f32[64,3,2,64]{3,2,1,0:T(2,128)S(1)}, bf16[128,1024]{1,0:T(8,128)(2,1)S(1)}, f32[2,16]{1,0:T(2,128)S(1)}) custom-call(bf16[6,32,128]{2,1,0:T(8,128)(2,1)} %bitcast.10, bf16[216,8]{1,0:T(8,128)(2,1)} %bitcast.9, bf16[128,1024]{1,0:T(8,128)(2,1)} %bitcast.8, bf16[448,64]{1,0:T(8,128)(2,1)} %constant.2.clone.table_ref, s32[16]{0:T(128)} %src_ref.1, ...), custom_call_target="tpu_custom_call" | custom-call | tf_op jit(solution)/shard_map/pallas_call | solution.py:497
  31.2 0.8 %shard_map.95 = (f32[64,3,2,64]{3,2,1,0:T(2,128)}, bf16[128,1024]{1,0:T(8,128)(2,1)}, f32[2,16]{1,0:T(2,128)}) custom-call(f32[64,3,2,64]{3,2,1,0:T(2,128)S(1)} %get-tuple-element.9.refs_0_, bf16[128,1024]{1,0:T(8,128)(2,1)S(1)} %get-tuple-element.10.refs_1_, f32[2,16]{1,0:T(2,128)S(1)} %get-tuple-element.11.refs_2_), custom_call_target="tpu_custom_call" | custom-call | tf_op jit(solution)/shard_map/pallas_call | solution.py:537
